TPU v7x, 32 devices: a whole 2x2x4 slice. The times are simulated.
32 devices in a mesh: dp: 16 (over z, y, x), space: 2 (over core).
Axes of the slice: x: 2, y: 2, z: 4, core: 2. Of those that a mesh axis runs over, the one named last changes fastest.
Arguments:
- images: bfloat16 [16, 16, 288, 256], P('dp', 'space'), may hold values from -12 to 12
- w_reduce: bfloat16 [256, 64], replicated, may hold values from -0.375 to 0.375
- w_dilated: bfloat16 [3, 3, 64, 64], replicated, may hold values from -0.25 to 0.25
- w_expand: bfloat16 [64, 256], replicated, may hold values from -0.75 to 0.75
- gain_one: float32 [64], replicated, may hold values from 0.25 to 1.75
- shift_one: float32 [64], replicated, may hold values from -3 to 3
- gain_two: float32 [64], replicated, may hold values from 0.25 to 1.75
- shift_two: float32 [64], replicated, may hold values from -3 to 3
- gain_three: float32 [256], replicated, may hold values from 0.25 to 1.75
- shift_three: float32 [256], replicated, may hold values from -3 to 3
- cotangent: bfloat16 [16, 16, 288, 256], P('dp', 'space'), may hold values from -6 to 6
Outputs:
- result: bfloat16 [16, 16, 288, 256], P('dp', 'space')
- grad_images: bfloat16 [16, 16, 288, 256], P('dp', 'space')
- grad_reduce: float32 [256, 64], replicated
- grad_dilated: float32 [3, 3, 64, 64], replicated
- grad_expand: float32 [64, 256], replicated
- grad_gain_one: float32 [64], replicated
- grad_shift_one: float32 [64], replicated
- grad_gain_two: float32 [64], replicated
- grad_shift_two: float32 [64], replicated
- grad_gain_three: float32 [256], replicated
- grad_shift_three: float32 [256], replicated
All inputs are finite; a program needn't handle non-finite values.
Results may differ from a plain program's by a relative error of at most 0.012.
Values may be sent and summed in bfloat16 or wider, within the bound.
No kernel may reach another device: no remote copies, remote signals or barrier semaphores. Data moves between devices by JAX's collectives and lax.ppermute only.
A program may use at most 64 MiB of HBM per device.

v0:
```python
import jax
import jax.numpy as jnp
from jax import lax
from jax.sharding import PartitionSpec as P

epsilon = 1e-05


def extended(block, sides, width):
    for axis, dim in sides:
        count = lax.axis_size(axis)
        forward = [(i, i + 1) for i in range(count - 1)]
        backward = [(target, source) for source, target in forward]
        low = lax.ppermute(
            lax.slice_in_dim(block, block.shape[dim] - width, None, axis=dim), axis, forward
        )
        high = lax.ppermute(lax.slice_in_dim(block, 0, width, axis=dim), axis, backward)
        block = jnp.concatenate([low, block, high], axis=dim)
    return block


def smooth_act(value):
    return value * jax.nn.sigmoid(value)


def smooth_slope(value):
    sig = jax.nn.sigmoid(value)
    return sig * (1.0 + value * (1.0 - sig))


def normalize(pre, gain, shift, count):
    average = lax.psum(jnp.sum(pre, 0), "space") / count
    centred = pre - average
    variance = lax.psum(jnp.sum(centred * centred, 0), "space") / count
    inv_std = lax.rsqrt(variance + epsilon)
    normed = centred * inv_std
    return (normed, inv_std, gain * normed + shift)


def backnorm(grad, normed, inv_std, gain, count):
    local_sum = jnp.sum(grad, 0)
    local_cross = jnp.sum(grad * normed, 0)
    grad_sum, grad_cross = lax.psum((local_sum, local_cross), "space")
    back = (gain * inv_std * (grad - grad_sum / count - normed * grad_cross / count)).astype(
        jnp.bfloat16
    )
    return (back, local_cross, local_sum)


def dilated(padded, kernel, rows, cols):
    output = jnp.zeros((rows * cols, kernel.shape[3]), jnp.float32)
    for tap_row in range(3):
        for tap_col in range(3):
            window = padded[
                2 * tap_row : 2 * tap_row + rows, 2 * tap_col : 2 * tap_col + cols
            ].reshape(rows * cols, -1)
            output = output + jnp.dot(
                window, kernel[tap_row, tap_col], preferred_element_type=jnp.float32
            )
    return output


def contract(left, right):
    return lax.dot_general(
        left, right, (((0,), (0,)), ((), ())), preferred_element_type=jnp.float32
    )


def shards(
    images,
    w_reduce,
    w_dilated,
    w_expand,
    gain_one,
    shift_one,
    gain_two,
    shift_two,
    gain_three,
    shift_three,
    cotangent,
):
    rows, cols, chans = (images.shape[1], images.shape[2], images.shape[3])
    mids = w_reduce.shape[1]
    pixels = rows * cols
    count = float(pixels * lax.axis_size("space"))
    flat_in = images.reshape(pixels, chans)
    pre_one = jnp.dot(flat_in, w_reduce, preferred_element_type=jnp.float32)
    normed_one, istd_one, out_one = normalize(pre_one, gain_one, shift_one, count)
    act_one = smooth_act(out_one).astype(jnp.bfloat16)
    edged_one = extended(act_one.reshape(rows, cols, mids), (("space", 0),), 2)
    padded_one = jnp.pad(edged_one, ((0, 0), (2, 2), (0, 0)))
    pre_two = dilated(padded_one, w_dilated, rows, cols)
    normed_two, istd_two, out_two = normalize(pre_two, gain_two, shift_two, count)
    act_two = smooth_act(out_two).astype(jnp.bfloat16)
    pre_three = jnp.dot(act_two, w_expand, preferred_element_type=jnp.float32)
    normed_three, istd_three, out_three = normalize(pre_three, gain_three, shift_three, count)
    summed = out_three + flat_in.astype(jnp.float32)
    result = smooth_act(summed).astype(jnp.bfloat16)
    grad_three = cotangent.reshape(pixels, chans).astype(jnp.float32) * smooth_slope(summed)
    dh_three, gg_three, gs_three = backnorm(grad_three, normed_three, istd_three, gain_three, count)
    gw_expand = contract(act_two, dh_three)
    back_two = lax.dot_general(
        dh_three, w_expand, (((1,), (1,)), ((), ())), preferred_element_type=jnp.float32
    )
    grad_two = back_two * smooth_slope(out_two)
    dh_two, gg_two, gs_two = backnorm(grad_two, normed_two, istd_two, gain_two, count)
    taps = []
    for tap_row in range(3):
        for tap_col in range(3):
            window = padded_one[
                2 * tap_row : 2 * tap_row + rows, 2 * tap_col : 2 * tap_col + cols
            ].reshape(pixels, mids)
            taps.append(contract(window, dh_two))
    gw_dilated = jnp.stack(taps).reshape(3, 3, mids, mids)
    edged_back = extended(dh_two.reshape(rows, cols, mids), (("space", 0),), 2)
    padded_back = jnp.pad(edged_back, ((0, 0), (2, 2), (0, 0)))
    flipped = jnp.transpose(w_dilated[::-1, ::-1], (0, 1, 3, 2))
    grad_one = dilated(padded_back, flipped, rows, cols) * smooth_slope(out_one)
    dh_one, gg_one, gs_one = backnorm(grad_one, normed_one, istd_one, gain_one, count)
    gw_reduce = contract(flat_in, dh_one)
    back_in = lax.dot_general(
        dh_one, w_reduce, (((1,), (1,)), ((), ())), preferred_element_type=jnp.float32
    )
    grad_images = (back_in + grad_three).astype(jnp.bfloat16).reshape(1, rows, cols, chans)
    batch = float(lax.axis_size("dp"))
    parts_list = (
        gw_reduce,
        gw_dilated,
        gw_expand,
        gg_one,
        gs_one,
        gg_two,
        gs_two,
        gg_three,
        gs_three,
    )
    flat_grads = jnp.concatenate([item.reshape(-1) for item in parts_list])
    length = flat_grads.shape[0]
    groups = lax.axis_size("space")
    padded_len = (length + groups - 1) // groups * groups
    flat_grads = jnp.pad(flat_grads, (0, padded_len - length))
    share = lax.psum_scatter(
        flat_grads.astype(jnp.bfloat16), "space", scatter_dimension=0, tiled=True
    ).astype(jnp.float32)
    share = lax.psum(share, "dp")
    whole = lax.all_gather(share.astype(jnp.bfloat16), "space", axis=0, tiled=True).astype(
        share.dtype
    )
    summed_parts = []
    offset = 0
    for item in parts_list:
        summed_parts.append(whole[offset : offset + item.size].reshape(item.shape))
        offset = offset + item.size
    grads = [item / batch for item in summed_parts]
    return (
        result.reshape(1, rows, cols, chans),
        grad_images,
        grads[0],
        grads[1],
        grads[2],
        grads[3],
        grads[4],
        grads[5],
        grads[6],
        grads[7],
        grads[8],
    )


def solution(mesh):
    placed = (
        P("dp", "space", None, None),
        P(),
        P(),
        P(),
        P(),
        P(),
        P(),
        P(),
        P(),
        P(),
        P("dp", "space", None, None),
    )
    return jax.shard_map(
        shards,
        mesh=mesh,
        in_specs=placed,
        out_specs=(
            P("dp", "space", None, None),
            P("dp", "space", None, None),
            P(),
            P(),
            P(),
            P(),
            P(),
            P(),
            P(),
            P(),
            P(),
        ),
        check_vma=False,
    )
```

profile of v0, /device:TPU:0, one launch (start us, length us, event | category | flops | bytes accessed | tf_op | source)
XLA Modules:
  0.0 222.0 jit_solution(6507126635642277111)
XLA Ops:
  7.3 1.9 fusion.59
  9.2 2.6 %psum.91 = f32[64]{0:T(128)S(1)} all-reduce(f32[64]{0:T(128)S(1)} %get-tuple-element.81), channel_id=1, replica_groups=mesh['dp'=16,'space'=2] {'space'}, use_global_device_ids=true, to_apply=%region_1.0 | all-reduce | flops 64 | bytes 512 | tf_op jit(solution)/shard_map/psum | solution.py:32
  12.1 2.5 %psum.92 = f32[64]{0:T(128)S(1)} all-reduce(f32[64]{0:T(128)S(1)} %multiply_reduce_fusion.5), channel_id=1, replica_groups=mesh['dp'=16,'space'=2] {'space'}, use_global_device_ids=true, to_apply=%region_3.0 | all-reduce | flops 64 | bytes 512 | tf_op jit(solution)/shard_map/psum | solution.py:34
  16.3 2.3 %collective-permute-start = (bf16[2,288,64]{1,0,2:T(2,128)(2,1)S(1)}, bf16[2,288,64]{1,0,2:T(2,128)(2,1)S(1)}, u32[]{:S(2)}, u32[]{:S(2)}) collective-permute-start(bf16[2,288,64]{1,0,2:T(2,128)(2,1)S(1)} %slice.191), channel_id=1, source_target_pairs={{0,1},{2,3},{4,5},{6,7},{8,9},{10,11},{12,13},{14,15},{16,17},{18,... | collective-permute-start | bytes 221192 | tf_op jit(solution)/shard_map/ppermute | solution.py:14
  23.6 1.8 fusion.56
  42.2 3.3 %psum.93 = f32[64]{0:T(128)S(1)} all-reduce(f32[64]{0:T(128)S(1)} %get-tuple-element.83), channel_id=1, replica_groups=mesh['dp'=16,'space'=2] {'space'}, use_global_device_ids=true, to_apply=%region_5.6 | all-reduce | flops 64 | bytes 512 | tf_op jit(solution)/shard_map/psum | solution.py:32
  45.7 2.5 %psum.94 = f32[64]{0:T(128)S(1)} all-reduce(f32[64]{0:T(128)S(1)} %multiply_reduce_fusion.4), channel_id=1, replica_groups=mesh['dp'=16,'space'=2] {'space'}, use_global_device_ids=true, to_apply=%region_7.8 | all-reduce | flops 64 | bytes 512 | tf_op jit(solution)/shard_map/psum | solution.py:34
  48.2 1.9 fusion.61
  50.1 2.5 %psum.95 = f32[256]{0:T(256)S(1)} all-reduce(f32[256]{0:T(256)S(1)} %get-tuple-element.85), channel_id=1, replica_groups=mesh['dp'=16,'space'=2] {'space'}, use_global_device_ids=true, to_apply=%region_9.10 | all-reduce | flops 256 | bytes 2048 | tf_op jit(solution)/shard_map/psum | solution.py:32
  52.9 2.6 %psum.96 = f32[256]{0:T(256)S(1)} all-reduce(f32[256]{0:T(256)S(1)} %multiply_reduce_fusion.1), channel_id=1, replica_groups=mesh['dp'=16,'space'=2] {'space'}, use_global_device_ids=true, to_apply=%region_11.12 | all-reduce | flops 256 | bytes 2048 | tf_op jit(solution)/shard_map/psum | solution.py:34
  55.6 5.1 %fusion.52 = (f32[256]{0:T(256)S(1)}, f32[256]{0:T(256)S(1)}, f32[2304,256]{1,0:T(8,128)}, bf16[2304,256]{1,0:T(8,128)(2,1)}) fusion(f32[256]{0:T(256)S(1)} %get-tuple-element.76, f32[2304,256]{1,0:T(8,128)S(1)} %get-tuple-element.86, f32[256]{0:T(256)S(1)} %broadcast_multiply_fusion.1, bf16[1,8,288,256]{3,2,1,0:T(8,128)(2,1)} %param.11, ...), kind=kLoop, calls=%fused_computation.141 | loop fusion | flops 11795968 | bytes 8263680 | tf_op jit(solution)/shard_map/reduce_sum | solution.py:41
  60.6 2.5 %all-reduce.5 = (f32[256]{0:T(256)S(1)}, f32[256]{0:T(256)S(1)}) all-reduce(f32[256]{0:T(256)S(1)} %get-tuple-element.34, f32[256]{0:T(256)S(1)} %get-tuple-element.33), channel_id=1, replica_groups=mesh['dp'=16,'space'=2] {'space'}, use_global_device_ids=true, to_apply=%region_15.16 | all-reduce | flops 512 | bytes 4096 | tf_op jit(solution)/shard_map/psum | solution.py:43
  63.1 2.3 %multiply_convert_fusion = bf16[2304,256]{1,0:T(8,128)(2,1)S(1)} fusion(f32[2304,256]{1,0:T(8,128)} %get-tuple-element.45, f32[2304,256]{1,0:T(8,128)S(1)} %get-tuple-element.86, f32[256]{0:T(256)S(1)} %get-tuple-element.43, f32[256]{0:T(256)S(1)} %broadcast_multiply_fusion, f32[256]{0:T(256)S(1)} %get-tuple-element.75, f32[256]{0:T(256)S(1)} %get-tuple-element.76, ...), kind=kLoop, calls=%fused_computation.23 | loop fusion | flops 4718592 | bytes 5903360 | tf_op jit(solution)/shard_map/convert_element_type | solution.py:44
  67.3 2.6 %all-reduce.4 = (f32[64]{0:T(128)S(1)}, f32[64]{0:T(128)S(1)}) all-reduce(f32[64]{0:T(128)S(1)} %get-tuple-element.38, f32[64]{0:T(128)S(1)} %get-tuple-element.37), channel_id=1, replica_groups=mesh['dp'=16,'space'=2] {'space'}, use_global_device_ids=true, to_apply=%region_19.20 | all-reduce | flops 128 | bytes 1024 | tf_op jit(solution)/shard_map/psum | solution.py:43
  69.9 1.5 multiply_convert_fusion.3
  73.6 2.3 %collective-permute-start.2 = (bf16[2,288,64]{1,0,2:T(2,128)(2,1)S(1)}, bf16[2,288,64]{1,0,2:T(2,128)(2,1)S(1)}, u32[]{:S(2)}, u32[]{:S(2)}) collective-permute-start(bf16[2,288,64]{1,0,2:T(2,128)(2,1)S(1)} %slice.212), channel_id=1, source_target_pairs={{0,1},{2,3},{4,5},{6,7},{8,9},{10,11},{12,13},{14,15},{16,17},{18,... | collective-permute-start | bytes 221192 | tf_op jit(solution)/shard_map/ppermute | solution.py:14
  84.3 1.5 fusion.55
  94.8 3.6 %all-reduce.3 = (f32[64]{0:T(128)S(1)}, f32[64]{0:T(128)S(1)}) all-reduce(f32[64]{0:T(128)S(1)} %get-tuple-element.36, f32[64]{0:T(128)S(1)} %get-tuple-element.35), channel_id=1, replica_groups=mesh['dp'=16,'space'=2] {'space'}, use_global_device_ids=true, to_apply=%region_23.24 | all-reduce | flops 128 | bytes 1024 | tf_op jit(solution)/shard_map/psum | solution.py:43
  99.9 1.6 fusion.5
  101.7 6.3 %concatenate.28 = bf16[70400]{0:T(1024)(128)(2,1)} concatenate(bf16[16384]{0:T(1024)(128)(2,1)S(1)} %reshape.180, bf16[36864]{0:T(1024)(128)(2,1)S(1)} %copy-done.27, bf16[16384]{0:T(1024)(128)(2,1)S(1)} %bitcast.206, bf16[64]{0:T(256)(128)(2,1)S(1)} %convert.77, bf16[64]{0:T(256)(128)(2,1)S(1)} %convert.78, bf16[64]{0:T(256)(128)(2,1)S(1)} %copy-done.39, ...), dimensions={0} | concatenate | bytes 281600 | tf_op jit(solution)/shard_map/concatenate | solution.py:137
  108.1 1.5 fusion
  109.6 18.9 %all-reduce.9.cloned.1.call-done = bf16[70400]{0:T(1024)(128)(2,1)} async-done(((bf16[70400]{0:T(1024)(128)(2,1)}), bf16[70400]{0:T(1024)(128)(2,1)}) %all-reduce.9.cloned.1.call-update) | async-done | bytes 140816
  129.5 78.9 %all-reduce.10 = bf16[35200]{0:T(1024)(128)(2,1)S(1)} all-reduce(f32[35200]{0:T(1024)S(1)} %dynamic-slice_convert_fusion), channel_id=1, replica_groups=mesh['dp'=16,'space'=2] {'dp'}, use_global_device_ids=true, to_apply=%region_25.26 | all-reduce | flops 35200 | bytes 211200 | tf_op jit(solution)/shard_map/psum | solution.py:145
  208.5 2.0 all-gather
  (195 shorter events, 51.8 us)
Async XLA Ops:
  7.2 41.0 %copy-start = (bf16[64,256]{1,0:T(8,128)(2,1)S(1)}, bf16[64,256]{1,0:T(8,128)(2,1)}, u32[]{:S(2)}) copy-start(bf16[64,256]{1,0:T(8,128)(2,1)} %param.14) | copy-start | bytes 98308
  7.2 13.4 %copy-start.45 = (u32[32]{0:T(128)S(1)}, u32[32]{0:T(128)}, u32[]{:S(2)}) copy-start(u32[32]{0:T(128)} %constant.51) | copy-start | bytes 388
  7.2 7.3 %copy-start.34 = (f32[64]{0:T(128)S(1)}, f32[64]{0:T(128)}, u32[]{:S(2)}) copy-start(f32[64]{0:T(128)} %param.15) | copy-start | bytes 772
  7.2 8.4 %copy-start.37 = (f32[64]{0:T(128)S(1)}, f32[64]{0:T(128)}, u32[]{:S(2)}) copy-start(f32[64]{0:T(128)} %param.16) | copy-start | bytes 772
  7.2 14.6 %copy-start.25 = (bf16[3,3,64,64]{3,2,1,0:T(8,128)(2,1)S(1)}, bf16[3,3,64,64]{3,2,1,0:T(8,128)(2,1)}, u32[]{:S(2)}) copy-start(bf16[3,3,64,64]{3,2,1,0:T(8,128)(2,1)} %param.13) | copy-start | bytes 221188
  7.2 121.3 %all-reduce.9.cloned.1.call-start = ((), (), s32[]{:S(2)}) async-start(), calls=%async_computation | async-start | bytes 282624
  16.3 6.3 %collective-permute-start = (bf16[2,288,64]{1,0,2:T(2,128)(2,1)S(1)}, bf16[2,288,64]{1,0,2:T(2,128)(2,1)S(1)}, u32[]{:S(2)}, u32[]{:S(2)}) collective-permute-start(bf16[2,288,64]{1,0,2:T(2,128)(2,1)S(1)} %slice.191), channel_id=1, source_target_pairs={{0,1},{2,3},{4,5},{6,7},{8,9},{10,11},{12,13},{14,15},{16,17},{18,... | collective-permute-start | bytes 221192 | tf_op jit(solution)/shard_map/ppermute | solution.py:14
  18.7 3.9 %collective-permute-start.1 = (bf16[2,288,64]{1,0,2:T(2,128)(2,1)S(1)}, bf16[2,288,64]{1,0,2:T(2,128)(2,1)S(1)}, u32[]{:S(2)}, u32[]{:S(2)}) collective-permute-start(bf16[2,288,64]{1,0,2:T(2,128)(2,1)S(1)} %slice.193), channel_id=1, source_target_pairs={{1,0},{3,2},{5,4},{7,6},{9,8},{11,10},{13,12},{15,14},{17,16},{19,... | collective-permute-start | bytes 221192 | tf_op jit(solution)/shard_map/ppermute | solution.py:17
  25.7 5.7 %copy-start.9 = (bf16[2304,64]{0,1:T(8,128)(2,1)}, bf16[2304,64]{0,1:T(8,128)(2,1)S(1)}, u32[]{:S(2)}) copy-start(bf16[2304,64]{0,1:T(8,128)(2,1)S(1)} %reshape.161) | copy-start | bytes 884740
  27.5 6.1 %copy-start.15 = (bf16[2304,64]{0,1:T(8,128)(2,1)}, bf16[2304,64]{0,1:T(8,128)(2,1)S(1)}, u32[]{:S(2)}) copy-start(bf16[2304,64]{0,1:T(8,128)(2,1)S(1)} %reshape.162) | copy-start | bytes 884740
  40.0 8.2 %copy-start.43 = (f32[64]{0:T(128)S(1)}, f32[64]{0:T(128)}, u32[]{:S(2)}) copy-start(f32[64]{0:T(128)} %param.17) | copy-start | bytes 772
  40.0 8.2 %copy-start.44 = (f32[64]{0:T(128)S(1)}, f32[64]{0:T(128)}, u32[]{:S(2)}) copy-start(f32[64]{0:T(128)} %param.18) | copy-start | bytes 772
  42.2 6.0 %copy-start.2 = (f32[2304,64]{0,1:T(8,128)}, f32[2304,64]{0,1:T(8,128)S(1)}, u32[]{:S(2)}) copy-start(f32[2304,64]{0,1:T(8,128)S(1)} %get-tuple-element.84) | copy-start | bytes 1769476
  48.2 7.4 %copy-start.33 = (f32[256]{0:T(256)S(1)}, f32[256]{0:T(256)}, u32[]{:S(2)}) copy-start(f32[256]{0:T(256)} %param.19) | copy-start | bytes 3076
  48.2 7.4 %copy-start.36 = (f32[256]{0:T(256)S(1)}, f32[256]{0:T(256)}, u32[]{:S(2)}) copy-start(f32[256]{0:T(256)} %param.20) | copy-start | bytes 3076
  73.6 7.4 %collective-permute-start.2 = (bf16[2,288,64]{1,0,2:T(2,128)(2,1)S(1)}, bf16[2,288,64]{1,0,2:T(2,128)(2,1)S(1)}, u32[]{:S(2)}, u32[]{:S(2)}) collective-permute-start(bf16[2,288,64]{1,0,2:T(2,128)(2,1)S(1)} %slice.212), channel_id=1, source_target_pairs={{0,1},{2,3},{4,5},{6,7},{8,9},{10,11},{12,13},{14,15},{16,17},{18,... | collective-permute-start | bytes 221192 | tf_op jit(solution)/shard_map/ppermute | solution.py:14
  76.0 5.0 %collective-permute-start.3 = (bf16[2,288,64]{1,0,2:T(2,128)(2,1)S(1)}, bf16[2,288,64]{1,0,2:T(2,128)(2,1)S(1)}, u32[]{:S(2)}, u32[]{:S(2)}) collective-permute-start(bf16[2,288,64]{1,0,2:T(2,128)(2,1)S(1)} %slice.214), channel_id=1, source_target_pairs={{1,0},{3,2},{5,4},{7,6},{9,8},{11,10},{13,12},{15,14},{17,16},{19,... | collective-permute-start | bytes 221192 | tf_op jit(solution)/shard_map/ppermute | solution.py:17
  94.7 7.0 %copy-start.27 = (bf16[36864]{0:T(1024)(128)(2,1)S(1)}, bf16[36864]{0:T(1024)(128)(2,1)}, u32[]{:S(2)}) copy-start(bf16[36864]{0:T(1024)(128)(2,1)} %reshape_reshape.4) | copy-start | bytes 221188
  94.7 7.0 %copy-start.39 = (bf16[64]{0:T(256)(128)(2,1)S(1)}, bf16[64]{0:T(256)(128)(2,1)}, u32[]{:S(2)}) copy-start(bf16[64]{0:T(256)(128)(2,1)} %convert.79) | copy-start | bytes 388
  94.7 7.0 %copy-start.40 = (bf16[64]{0:T(256)(128)(2,1)S(1)}, bf16[64]{0:T(256)(128)(2,1)}, u32[]{:S(2)}) copy-start(bf16[64]{0:T(256)(128)(2,1)} %convert.80) | copy-start | bytes 388
  94.7 7.0 %copy-start.41 = (bf16[256]{0:T(256)(128)(2,1)S(1)}, bf16[256]{0:T(256)(128)(2,1)}, u32[]{:S(2)}) copy-start(bf16[256]{0:T(256)(128)(2,1)} %convert.81) | copy-start | bytes 1540
  94.8 7.0 %copy-start.42 = (bf16[256]{0:T(256)(128)(2,1)S(1)}, bf16[256]{0:T(256)(128)(2,1)}, u32[]{:S(2)}) copy-start(bf16[256]{0:T(256)(128)(2,1)} %convert.82) | copy-start | bytes 1540
  94.8 13.3 %copy-start.1 = (f32[2304,256]{1,0:T(8,128)S(1)}, f32[2304,256]{1,0:T(8,128)}, u32[]{:S(2)}) copy-start(f32[2304,256]{1,0:T(8,128)} %get-tuple-element.45) | copy-start | bytes 7077892
  94.8 13.3 %copy-start.28 = (bf16[256,64]{0,1:T(8,128)(2,1)S(1)}, bf16[256,64]{0,1:T(8,128)(2,1)}, u32[]{:S(2)}) copy-start(bf16[256,64]{0,1:T(8,128)(2,1)} %param.12) | copy-start | bytes 98308
  (27 other events, 85.6 us)
Sparse Core Ops, SparseCore 0:
  108.2 20.3 all-reduce.8
where the time goes:
time: 223 us; the launch traced here: 222 us
  blocking collectives  106 us (48%)
  local copies, waits for them, and re-layouts  29.5 us (13%)
  matrix products  23.4 us (10%)
  other arithmetic  21.6 us (10%)
  waiting for transfers between devices  19 us (9%)
  between operations  15.8 us (7%)
  starting transfers between devices  7.13 us (3%)
    psum x1, blocking collectives, shards(): share = lax.psum(share, 'dp')  78.9 us
    unnamed x2, waiting for transfers between devices  19 us
    dot_general x18, matrix products, dilated(): jnp.dot(window, kernel[tap_row, tap_col], preferred_element_type=jnp.floa...  12.7 us
    reshape x16, local copies, waits for them, and re-layouts, dilated(): window = padded[2 * tap_row:2 * tap_row + rows, 2 * tap_col:2 * tap_col +...  12.4 us
    psum x3, blocking collectives, backnorm(): grad_sum, grad_cross = lax.psum((local_sum, local_cross), 'space')  8.68 us
    psum x3, blocking collectives, normalize(): average = lax.psum(jnp.sum(pre, 0), 'space') / count  8.36 us
    psum x3, blocking collectives, normalize(): variance = lax.psum(jnp.sum(centred * centred, 0), 'space') / count  7.59 us
    concatenate x1, local copies, waits for them, and re-layouts, shards(): flat_grads = jnp.concatenate([item.reshape(-1) for item in parts_list])  6.29 us
  transfers between devices with their start and end apart: 5, of which 1 were waited for; matrix products, arithmetic and copies ran while one was open for 3% of the time, Pallas kernels for 0%

commit v1 on v0

--- a/solution.py
+++ b/solution.py
@@ -4,6 +4,11 @@
 from jax.sharding import PartitionSpec as P
 
 epsilon = 1e-05
+
+
+def add_all(block, name):
+    shards = lax.all_gather(block, name)
+    return jnp.sum(shards, axis=0)
 
 
 def extended(block, sides, width):
@@ -142,7 +147,7 @@
     share = lax.psum_scatter(
         flat_grads.astype(jnp.bfloat16), "space", scatter_dimension=0, tiled=True
     ).astype(jnp.float32)
-    share = lax.psum(share, "dp")
+    share = add_all(share, "dp")
     whole = lax.all_gather(share.astype(jnp.bfloat16), "space", axis=0, tiled=True).astype(
         share.dtype
     )

time: 223 us -> 212 us (0.951)
  blocking collectives: 106 us -> 25.8 us
  waiting for transfers between devices: 19 us -> 82.5 us
  other arithmetic: 21.6 us -> 24.6 us
    psum x1 -> x0, blocking collectives: 78.9 us -> none  [shards(): share = lax.psum(share, 'dp')]
    all_gather x0 -> x1, waiting for transfers between devices: none -> 62.7 us  [add_all(): shards = lax.all_gather(block, name)]
    reduce_sum x0 -> x1, other arithmetic: none -> 3.03 us  [add_all(): return jnp.sum(shards, axis=0)]
    unnamed x2 -> x3, waiting for transfers between devices: 19 us -> 19.2 us
  transfers between devices with their start and end apart: 5 -> 6, of which waited for: 1 -> 3; matrix products, arithmetic and copies ran while one was open for 3% -> 3% of each run, Pallas kernels for 0% -> 0%
where the time goes in v1:
time: 212 us; the launch traced here: 210 us
  waiting for transfers between devices  82.5 us (39%)
  local copies, waits for them, and re-layouts  31.1 us (15%)
  blocking collectives  25.8 us (12%)
  other arithmetic  24.6 us (12%)
  matrix products  23.4 us (11%)
  between operations  15.8 us (7%)
  starting transfers between devices  7.17 us (3%)
    all_gather x1, waiting for transfers between devices, add_all(): shards = lax.all_gather(block, name)  62.7 us
    unnamed x3, waiting for transfers between devices  19.2 us
    reshape x16, local copies, waits for them, and re-layouts, dilated(): window = padded[2 * tap_row:2 * tap_row + rows, 2 * tap_col:2 * tap_col +...  13.2 us
    dot_general x18, matrix products, dilated(): jnp.dot(window, kernel[tap_row, tap_col], preferred_element_type=jnp.floa...  12.7 us
    psum x3, blocking collectives, backnorm(): grad_sum, grad_cross = lax.psum((local_sum, local_cross), 'space')  8.45 us
    psum x3, blocking collectives, normalize(): average = lax.psum(jnp.sum(pre, 0), 'space') / count  7.77 us
    psum x3, blocking collectives, normalize(): variance = lax.psum(jnp.sum(centred * centred, 0), 'space') / count  7.59 us
    concatenate x1, local copies, waits for them, and re-layouts, shards(): flat_grads = jnp.concatenate([item.reshape(-1) for item in parts_list])  6.29 us
  transfers between devices with their start and end apart: 6, of which 3 were waited for; matrix products, arithmetic and copies ran while one was open for 3% of the time, Pallas kernels for 0%

profile of v1, /device:TPU:0, one launch (start us, length us, event | category | flops | bytes accessed | tf_op | source)
XLA Modules:
  0.0 210.4 jit_solution(5421898446842134675)
XLA Ops:
  7.3 1.9 fusion.59
  9.2 2.6 %psum.84 = f32[64]{0:T(128)S(1)} all-reduce(f32[64]{0:T(128)S(1)} %get-tuple-element.81), channel_id=1, replica_groups=mesh['dp'=16,'space'=2] {'space'}, use_global_device_ids=true, to_apply=%region_1.0 | all-reduce | flops 64 | bytes 512 | tf_op jit(solution)/shard_map/psum | solution.py:37
  12.1 2.5 %psum.85 = f32[64]{0:T(128)S(1)} all-reduce(f32[64]{0:T(128)S(1)} %multiply_reduce_fusion.5), channel_id=1, replica_groups=mesh['dp'=16,'space'=2] {'space'}, use_global_device_ids=true, to_apply=%region_3.0 | all-reduce | flops 64 | bytes 512 | tf_op jit(solution)/shard_map/psum | solution.py:39
  16.3 2.3 %collective-permute-start = (bf16[2,288,64]{1,0,2:T(2,128)(2,1)S(1)}, bf16[2,288,64]{1,0,2:T(2,128)(2,1)S(1)}, u32[]{:S(2)}, u32[]{:S(2)}) collective-permute-start(bf16[2,288,64]{1,0,2:T(2,128)(2,1)S(1)} %slice.191), channel_id=1, source_target_pairs={{0,1},{2,3},{4,5},{6,7},{8,9},{10,11},{12,13},{14,15},{16,17},{18,... | collective-permute-start | bytes 221192 | tf_op jit(solution)/shard_map/ppermute | solution.py:19
  22.9 1.8 fusion.56
  41.6 2.7 %psum.86 = f32[64]{0:T(128)S(1)} all-reduce(f32[64]{0:T(128)S(1)} %get-tuple-element.83), channel_id=1, replica_groups=mesh['dp'=16,'space'=2] {'space'}, use_global_device_ids=true, to_apply=%region_5.6 | all-reduce | flops 64 | bytes 512 | tf_op jit(solution)/shard_map/psum | solution.py:37
  44.5 2.5 %psum.87 = f32[64]{0:T(128)S(1)} all-reduce(f32[64]{0:T(128)S(1)} %multiply_reduce_fusion.4), channel_id=1, replica_groups=mesh['dp'=16,'space'=2] {'space'}, use_global_device_ids=true, to_apply=%region_7.8 | all-reduce | flops 64 | bytes 512 | tf_op jit(solution)/shard_map/psum | solution.py:39
  47.1 1.9 fusion.61
  48.9 2.5 %psum.88 = f32[256]{0:T(256)S(1)} all-reduce(f32[256]{0:T(256)S(1)} %get-tuple-element.85), channel_id=1, replica_groups=mesh['dp'=16,'space'=2] {'space'}, use_global_device_ids=true, to_apply=%region_9.10 | all-reduce | flops 256 | bytes 2048 | tf_op jit(solution)/shard_map/psum | solution.py:37
  51.8 2.6 %psum.89 = f32[256]{0:T(256)S(1)} all-reduce(f32[256]{0:T(256)S(1)} %multiply_reduce_fusion.1), channel_id=1, replica_groups=mesh['dp'=16,'space'=2] {'space'}, use_global_device_ids=true, to_apply=%region_11.12 | all-reduce | flops 256 | bytes 2048 | tf_op jit(solution)/shard_map/psum | solution.py:39
  54.4 5.1 %fusion.52 = (f32[256]{0:T(256)S(1)}, f32[256]{0:T(256)S(1)}, f32[2304,256]{1,0:T(8,128)}, bf16[2304,256]{1,0:T(8,128)(2,1)}) fusion(f32[256]{0:T(256)S(1)} %get-tuple-element.76, f32[2304,256]{1,0:T(8,128)S(1)} %get-tuple-element.86, f32[256]{0:T(256)S(1)} %broadcast_multiply_fusion.1, bf16[1,8,288,256]{3,2,1,0:T(8,128)(2,1)} %param.11, ...), kind=kLoop, calls=%fused_computation.141 | loop fusion | flops 11795968 | bytes 8263680 | tf_op jit(solution)/shard_map/reduce_sum | solution.py:46
  59.5 2.5 %all-reduce.5 = (f32[256]{0:T(256)S(1)}, f32[256]{0:T(256)S(1)}) all-reduce(f32[256]{0:T(256)S(1)} %get-tuple-element.34, f32[256]{0:T(256)S(1)} %get-tuple-element.33), channel_id=1, replica_groups=mesh['dp'=16,'space'=2] {'space'}, use_global_device_ids=true, to_apply=%region_15.16 | all-reduce | flops 512 | bytes 4096 | tf_op jit(solution)/shard_map/psum | solution.py:48
  61.9 2.3 %multiply_convert_fusion = bf16[2304,256]{1,0:T(8,128)(2,1)S(1)} fusion(f32[2304,256]{1,0:T(8,128)} %get-tuple-element.45, f32[2304,256]{1,0:T(8,128)S(1)} %get-tuple-element.86, f32[256]{0:T(256)S(1)} %get-tuple-element.43, f32[256]{0:T(256)S(1)} %broadcast_multiply_fusion, f32[256]{0:T(256)S(1)} %get-tuple-element.75, f32[256]{0:T(256)S(1)} %get-tuple-element.76, ...), kind=kLoop, calls=%fused_computation.23 | loop fusion | flops 4718592 | bytes 5903360 | tf_op jit(solution)/shard_map/convert_element_type | solution.py:49
  66.2 2.6 %all-reduce.4 = (f32[64]{0:T(128)S(1)}, f32[64]{0:T(128)S(1)}) all-reduce(f32[64]{0:T(128)S(1)} %get-tuple-element.38, f32[64]{0:T(128)S(1)} %get-tuple-element.37), channel_id=1, replica_groups=mesh['dp'=16,'space'=2] {'space'}, use_global_device_ids=true, to_apply=%region_19.20 | all-reduce | flops 128 | bytes 1024 | tf_op jit(solution)/shard_map/psum | solution.py:48
  72.5 2.3 %collective-permute-start.2 = (bf16[2,288,64]{1,0,2:T(2,128)(2,1)S(1)}, bf16[2,288,64]{1,0,2:T(2,128)(2,1)S(1)}, u32[]{:S(2)}, u32[]{:S(2)}) collective-permute-start(bf16[2,288,64]{1,0,2:T(2,128)(2,1)S(1)} %slice.212), channel_id=1, source_target_pairs={{0,1},{2,3},{4,5},{6,7},{8,9},{10,11},{12,13},{14,15},{16,17},{18,... | collective-permute-start | bytes 221192 | tf_op jit(solution)/shard_map/ppermute | solution.py:19
  83.1 1.5 fusion.55
  94.3 3.4 %all-reduce.3 = (f32[64]{0:T(128)S(1)}, f32[64]{0:T(128)S(1)}) all-reduce(f32[64]{0:T(128)S(1)} %get-tuple-element.36, f32[64]{0:T(128)S(1)} %get-tuple-element.35), channel_id=1, replica_groups=mesh['dp'=16,'space'=2] {'space'}, use_global_device_ids=true, to_apply=%region_23.24 | all-reduce | flops 128 | bytes 1024 | tf_op jit(solution)/shard_map/psum | solution.py:48
  99.2 1.6 fusion.5
  101.1 6.3 %concatenate.28 = bf16[70400]{0:T(1024)(128)(2,1)} concatenate(bf16[16384]{0:T(1024)(128)(2,1)S(1)} %reshape.180, bf16[36864]{0:T(1024)(128)(2,1)S(1)} %copy-done.27, bf16[16384]{0:T(1024)(128)(2,1)S(1)} %bitcast.206, bf16[64]{0:T(256)(128)(2,1)S(1)} %convert.78, bf16[64]{0:T(256)(128)(2,1)S(1)} %convert.79, bf16[64]{0:T(256)(128)(2,1)S(1)} %copy-done.40, ...), dimensions={0} | concatenate | bytes 281600 | tf_op jit(solution)/shard_map/concatenate | solution.py:142
  108.7 19.2 %all-reduce.8.cloned.1.call-done = bf16[70400]{0:T(1024)(128)(2,1)} async-done(((bf16[70400]{0:T(1024)(128)(2,1)}), bf16[70400]{0:T(1024)(128)(2,1)}) %all-reduce.8.cloned.1.call-update) | async-done | bytes 140816
  129.7 1.5 fusion
  131.2 62.7 %all-gather.5.cloned.1.call-done = f32[16,1,35200]{2,1,0:T(1,128)} async-done(((f32[1,1,35200]{2,1,0:T(1,128)}), f32[16,1,35200]{2,1,0:T(1,128)}) %all-gather.5.cloned.1.call-update) | async-done | bytes 2252816 | tf_op jit(solution)/shard_map/all_gather | solution.py:10
  193.9 3.0 %reduce_sum.129 = bf16[35200]{0:T(1024)(128)(2,1)S(1)} reduce(f32[16,1,35200]{2,1,0:T(1,128)} %all-gather.5.cloned.1.call-done, f32[]{:T(128)} %constant.37.clone.1), dimensions={0,1}, to_apply=%region_25.26 | reduce | flops 528000 | bytes 2323204 | tf_op jit(solution)/shard_map/reduce_sum | solution.py:11
  197.0 2.0 all-gather.2
  (201 shorter events, 55.5 us)
Async XLA Ops:
  7.2 39.9 %copy-start = (bf16[64,256]{1,0:T(8,128)(2,1)S(1)}, bf16[64,256]{1,0:T(8,128)(2,1)}, u32[]{:S(2)}) copy-start(bf16[64,256]{1,0:T(8,128)(2,1)} %param.14) | copy-start | bytes 98308
  7.2 7.3 %copy-start.35 = (f32[64]{0:T(128)S(1)}, f32[64]{0:T(128)}, u32[]{:S(2)}) copy-start(f32[64]{0:T(128)} %param.15) | copy-start | bytes 772
  7.2 8.4 %copy-start.38 = (f32[64]{0:T(128)S(1)}, f32[64]{0:T(128)}, u32[]{:S(2)}) copy-start(f32[64]{0:T(128)} %param.16) | copy-start | bytes 772
  7.2 13.4 %copy-start.25 = (bf16[3,3,64,64]{3,2,1,0:T(8,128)(2,1)S(1)}, bf16[3,3,64,64]{3,2,1,0:T(8,128)(2,1)}, u32[]{:S(2)}) copy-start(bf16[3,3,64,64]{3,2,1,0:T(8,128)(2,1)} %param.13) | copy-start | bytes 221188
  7.2 120.6 %all-reduce.8.cloned.1.call-start = ((), (), s32[]{:S(2)}) async-start(), calls=%async_computation.1 | async-start | bytes 282624
  16.3 5.0 %collective-permute-start = (bf16[2,288,64]{1,0,2:T(2,128)(2,1)S(1)}, bf16[2,288,64]{1,0,2:T(2,128)(2,1)S(1)}, u32[]{:S(2)}, u32[]{:S(2)}) collective-permute-start(bf16[2,288,64]{1,0,2:T(2,128)(2,1)S(1)} %slice.191), channel_id=1, source_target_pairs={{0,1},{2,3},{4,5},{6,7},{8,9},{10,11},{12,13},{14,15},{16,17},{18,... | collective-permute-start | bytes 221192 | tf_op jit(solution)/shard_map/ppermute | solution.py:19
  18.7 3.2 %collective-permute-start.1 = (bf16[2,288,64]{1,0,2:T(2,128)(2,1)S(1)}, bf16[2,288,64]{1,0,2:T(2,128)(2,1)S(1)}, u32[]{:S(2)}, u32[]{:S(2)}) collective-permute-start(bf16[2,288,64]{1,0,2:T(2,128)(2,1)S(1)} %slice.193), channel_id=1, source_target_pairs={{1,0},{3,2},{5,4},{7,6},{9,8},{11,10},{13,12},{15,14},{17,16},{19,... | collective-permute-start | bytes 221192 | tf_op jit(solution)/shard_map/ppermute | solution.py:22
  26.8 6.1 %copy-start.15 = (bf16[2304,64]{0,1:T(8,128)(2,1)}, bf16[2304,64]{0,1:T(8,128)(2,1)S(1)}, u32[]{:S(2)}) copy-start(bf16[2304,64]{0,1:T(8,128)(2,1)S(1)} %reshape.162) | copy-start | bytes 884740
  34.2 6.3 %copy-start.19 = (bf16[2304,64]{0,1:T(8,128)(2,1)}, bf16[2304,64]{0,1:T(8,128)(2,1)S(1)}, u32[]{:S(2)}) copy-start(bf16[2304,64]{0,1:T(8,128)(2,1)S(1)} %reshape.165) | copy-start | bytes 884740
  39.4 7.6 %copy-start.44 = (f32[64]{0:T(128)S(1)}, f32[64]{0:T(128)}, u32[]{:S(2)}) copy-start(f32[64]{0:T(128)} %param.17) | copy-start | bytes 772
  39.4 7.6 %copy-start.45 = (f32[64]{0:T(128)S(1)}, f32[64]{0:T(128)}, u32[]{:S(2)}) copy-start(f32[64]{0:T(128)} %param.18) | copy-start | bytes 772
  47.0 7.4 %copy-start.34 = (f32[256]{0:T(256)S(1)}, f32[256]{0:T(256)}, u32[]{:S(2)}) copy-start(f32[256]{0:T(256)} %param.19) | copy-start | bytes 3076
  47.1 7.4 %copy-start.37 = (f32[256]{0:T(256)S(1)}, f32[256]{0:T(256)}, u32[]{:S(2)}) copy-start(f32[256]{0:T(256)} %param.20) | copy-start | bytes 3076
  72.5 7.4 %collective-permute-start.2 = (bf16[2,288,64]{1,0,2:T(2,128)(2,1)S(1)}, bf16[2,288,64]{1,0,2:T(2,128)(2,1)S(1)}, u32[]{:S(2)}, u32[]{:S(2)}) collective-permute-start(bf16[2,288,64]{1,0,2:T(2,128)(2,1)S(1)} %slice.212), channel_id=1, source_target_pairs={{0,1},{2,3},{4,5},{6,7},{8,9},{10,11},{12,13},{14,15},{16,17},{18,... | collective-permute-start | bytes 221192 | tf_op jit(solution)/shard_map/ppermute | solution.py:19
  74.9 5.0 %collective-permute-start.3 = (bf16[2,288,64]{1,0,2:T(2,128)(2,1)S(1)}, bf16[2,288,64]{1,0,2:T(2,128)(2,1)S(1)}, u32[]{:S(2)}, u32[]{:S(2)}) collective-permute-start(bf16[2,288,64]{1,0,2:T(2,128)(2,1)S(1)} %slice.214), channel_id=1, source_target_pairs={{1,0},{3,2},{5,4},{7,6},{9,8},{11,10},{13,12},{15,14},{17,16},{19,... | collective-permute-start | bytes 221192 | tf_op jit(solution)/shard_map/ppermute | solution.py:22
  94.2 6.8 %copy-start.27 = (bf16[36864]{0:T(1024)(128)(2,1)S(1)}, bf16[36864]{0:T(1024)(128)(2,1)}, u32[]{:S(2)}) copy-start(bf16[36864]{0:T(1024)(128)(2,1)} %reshape_reshape.4) | copy-start | bytes 221188
  94.3 6.8 %copy-start.40 = (bf16[64]{0:T(256)(128)(2,1)S(1)}, bf16[64]{0:T(256)(128)(2,1)}, u32[]{:S(2)}) copy-start(bf16[64]{0:T(256)(128)(2,1)} %convert.80) | copy-start | bytes 388
  94.3 6.8 %copy-start.41 = (bf16[64]{0:T(256)(128)(2,1)S(1)}, bf16[64]{0:T(256)(128)(2,1)}, u32[]{:S(2)}) copy-start(bf16[64]{0:T(256)(128)(2,1)} %convert.81) | copy-start | bytes 388
  94.3 6.8 %copy-start.42 = (bf16[256]{0:T(256)(128)(2,1)S(1)}, bf16[256]{0:T(256)(128)(2,1)}, u32[]{:S(2)}) copy-start(bf16[256]{0:T(256)(128)(2,1)} %convert.82) | copy-start | bytes 1540
  94.3 6.8 %copy-start.43 = (bf16[256]{0:T(256)(128)(2,1)S(1)}, bf16[256]{0:T(256)(128)(2,1)}, u32[]{:S(2)}) copy-start(bf16[256]{0:T(256)(128)(2,1)} %convert.83) | copy-start | bytes 1540
  94.3 13.1 %copy-start.46 = (u32[32]{0:T(128)S(1)}, u32[32]{0:T(128)}, u32[]{:S(2)}) copy-start(u32[32]{0:T(128)} %constant.51) | copy-start | bytes 388
  94.3 35.3 %copy-start.1 = (f32[2304,256]{1,0:T(8,128)S(1)}, f32[2304,256]{1,0:T(8,128)}, u32[]{:S(2)}) copy-start(f32[2304,256]{1,0:T(8,128)} %get-tuple-element.45) | copy-start | bytes 7077892
  94.3 35.3 %copy-start.29 = (bf16[256,64]{0,1:T(8,128)(2,1)S(1)}, bf16[256,64]{0,1:T(8,128)(2,1)}, u32[]{:S(2)}) copy-start(bf16[256,64]{0,1:T(8,128)(2,1)} %param.12) | copy-start | bytes 98308
  107.4 86.5 %all-gather.5.cloned.1.call-start = ((), (), s32[]{:S(2)}) async-start(), calls=%async_computation | async-start | bytes 2393600 | tf_op jit(solution)/shard_map/all_gather | solution.py:10
  (29 other events, 91.9 us)
Sparse Core Ops, SparseCore 0:
  107.5 20.3 all-reduce.7
  131.2 62.6 all-gather.4
